TPU v7x, 512 devices: a whole 4x8x8 slice. The times are simulated.
512 devices in a mesh: leaf: 8 (over y), blk: 64 (over x, z, core).
Axes of the slice: x: 4, y: 8, z: 8, core: 2. Of those that a mesh axis runs over, the one named last changes fastest.
Arguments:
- right_sides: bfloat16 [8, 64, 4, 512, 32], P('leaf', 'blk'), may hold values from -6 to 6
- inverses: bfloat16 [8, 64, 4, 512, 512], P('leaf', 'blk')
- couplings: bfloat16 [8, 64, 3, 256, 512], P('leaf', 'blk'), may hold values from -0.25 to 0.25
- widths: int32 [8, 64, 4], P('leaf', 'blk'), may hold values from 1 to 4, as said below
- targets: int32 [3, 8, 64, 64], replicated, may hold values from 0 to 16383, as said below
Outputs:
- solution: bfloat16 [8, 64, 4, 512, 32], P('leaf', 'blk')
Inputs may be any that keep to these rules, and one draw needn't show every extreme that they name: `widths`: at every level some device has 4 live block units. `targets`: every piece names live rows of its target supernode. At level l, with partner group g XOR 2 ** (l % log2(8)), devices (g, j) and (partner, j) together send at most 3 pieces to owners of blk index d, counting both groups. For each such pair of groups there are one blk index h and one of the two groups such that every pair (g, j), (partner, j) sends exactly 3 pieces to index h of that group, all from one of its two devices.
All inputs are finite; a program needn't handle non-finite values.
Results may differ from a plain program's by a relative error of at most 0.012.
Values may be sent and summed in bfloat16 or wider, within the bound.
A program may use at most 64 MiB of HBM per device.

v0:
```python
import jax
import jax.numpy as jnp
from jax import lax
from jax.sharding import PartitionSpec as P

BLOCK = 128


def partner_2(array, axis, distance):
    return lax.ppermute(array, axis, [(i, i ^ 1 << distance) for i in range(lax.axis_size(axis))])


def plain_dot(left, right):
    return jnp.dot(left, right, preferred_element_type=jnp.float32)


def trans_dot(left, right):
    return lax.dot_general(
        left, right, (((0,), (0,)), ((), ())), preferred_element_type=jnp.float32
    )


def decode_codes(code_list, blk_count, place_count):
    side_bit = code_list // (blk_count * place_count)
    dest_blk = code_list // place_count % blk_count
    row_place = code_list % place_count
    return (side_bit, dest_blk, row_place)


def rank_pieces(dest_blk, valid):
    position = jnp.arange(dest_blk.shape[-1])
    earlier = position[:, None] < position[None, :]
    matches = (dest_blk[..., :, None] == dest_blk[..., None, :]) & valid[..., :, None] & earlier
    return jnp.sum(matches.astype(jnp.int32), axis=-2)


def send_matrix(dest_blk, rank, valid, slot_cap, slot_count):
    slot_of = dest_blk * slot_cap + rank
    chosen = (jnp.arange(slot_count)[:, None] == slot_of[None, :]) & valid[None, :]
    return chosen.astype(jnp.bfloat16)


def receive_matrix(rank, row_place, used, slot_cap, place_count):
    place_hot = ((row_place[:, :, None] == jnp.arange(place_count)) & used[:, :, None]).astype(
        jnp.float32
    )
    rank_hot = (rank[:, :, None] == jnp.arange(slot_cap)).astype(jnp.float32)
    layout = jnp.einsum("skq,skc->qsc", place_hot, rank_hot)
    return layout.reshape(place_count, -1).astype(jnp.bfloat16)


def pick_row(table, index):
    return lax.dynamic_index_in_dim(table, index, 0, keepdims=False)


def shards(right_sides, inverses, couplings, widths, targets):
    blk_count = lax.axis_size("blk")
    leaf_count = lax.axis_size("leaf")
    leaf_bits = leaf_count.bit_length() - 1
    group_index = lax.axis_index("leaf")
    owner_index = lax.axis_index("blk")
    right_side = right_sides[0, 0]
    inverse = inverses[0, 0]
    coupling = couplings[0, 0]
    live_blocks = widths[0, 0]
    levels, node_width, col_count = right_side.shape
    piece_count = targets.shape[3]
    piece_rows = coupling.shape[1] // piece_count
    place_count = node_width // piece_rows
    flat_width = piece_rows * col_count
    slot_cap = max(3, (2 * piece_count + blk_count - 1) // blk_count + 1)
    slot_count = blk_count * slot_cap
    row_index = jnp.arange(node_width)
    row_masks = [
        (row_index < live_blocks[level] * BLOCK).astype(jnp.float32)[:, None]
        for level in range(levels)
    ]
    forward = []
    routes = []
    incoming = None
    for level in range(levels):
        if level == 0:
            residual = right_side[0]
        else:
            residual = (right_side[level].astype(jnp.float32) - incoming).astype(jnp.bfloat16)
        solved = (row_masks[level] * plain_dot(inverse[level], residual)).astype(jnp.bfloat16)
        forward.append(solved)
        if level + 1 < levels:
            pieces = (
                plain_dot(coupling[level], solved)
                .astype(jnp.bfloat16)
                .reshape(piece_count, flat_width)
            )
            leaf_bit = level % leaf_bits
            partner = jnp.bitwise_xor(group_index, 1 << leaf_bit)
            own_table = pick_row(targets[level], group_index)
            pair_table = pick_row(targets[level], partner)
            own_side, own_dest, own_place = decode_codes(own_table, blk_count, place_count)
            pair_side, pair_dest, pair_place = decode_codes(pair_table, blk_count, place_count)
            mine_dest = pick_row(own_dest, owner_index)
            every_piece = jnp.ones(mine_dest.shape, bool)
            mine_rank = rank_pieces(mine_dest[None], every_piece[None])[0]
            sender = send_matrix(mine_dest, mine_rank, every_piece, slot_cap, slot_count)
            buffer = plain_dot(sender, pieces).astype(jnp.bfloat16)
            arrived_slots = lax.all_to_all(buffer, "blk", split_axis=0, concat_axis=0, tiled=True)
            partner_slots = partner_2(arrived_slots, "leaf", leaf_bit)
            every_row = jnp.ones(own_dest.shape, bool)
            own_rank = rank_pieces(own_dest, every_row)
            pair_rank = rank_pieces(pair_dest, every_row)
            own_take = receive_matrix(
                own_rank,
                own_place,
                (own_dest == owner_index) & (own_side == 0),
                slot_cap,
                place_count,
            )
            pair_take = receive_matrix(
                pair_rank,
                pair_place,
                (pair_dest == owner_index) & (pair_side == 1),
                slot_cap,
                place_count,
            )
            incoming = (
                plain_dot(own_take, arrived_slots) + plain_dot(pair_take, partner_slots)
            ).reshape(node_width, col_count)
            routes.append((sender, own_take, pair_take))
    solution = [None] * levels
    for level in reversed(range(levels)):
        if level + 1 == levels:
            back_side = forward[level]
        else:
            above_rows = solution[level + 1].reshape(place_count, flat_width)
            leaf_bit = level % leaf_bits
            sender, own_take, pair_take = routes[level]
            own_reply = trans_dot(own_take, above_rows)
            pair_reply = trans_dot(pair_take, above_rows).astype(jnp.bfloat16)
            handed = partner_2(pair_reply, "leaf", leaf_bit)
            merged = (own_reply + handed.astype(jnp.float32)).astype(jnp.bfloat16)
            returned = lax.all_to_all(merged, "blk", split_axis=0, concat_axis=0, tiled=True)
            gathered = trans_dot(sender, returned).astype(jnp.bfloat16)
            rows_in = gathered.reshape(piece_count * piece_rows, col_count)
            back_side = (
                forward[level].astype(jnp.float32) - trans_dot(coupling[level], rows_in)
            ).astype(jnp.bfloat16)
        masked = back_side * row_masks[level].astype(jnp.bfloat16)
        solution[level] = (row_masks[level] * trans_dot(inverse[level], masked)).astype(
            jnp.bfloat16
        )
    return jnp.stack(solution, axis=0)[None, None]


def solution(mesh):
    return jax.shard_map(
        shards,
        mesh=mesh,
        in_specs=(
            P("leaf", "blk", None, None, None),
            P("leaf", "blk", None, None, None),
            P("leaf", "blk", None, None, None),
            P("leaf", "blk", None),
            P(),
        ),
        out_specs=P("leaf", "blk", None, None, None),
        check_vma=False,
    )
```

profile of v0, /device:TPU:1, one launch (start us, length us, event | category | flops | bytes accessed | tf_op | source)
XLA Modules:
  0.0 183.2 jit_solution(8884602952059697542)
XLA Ops:
  7.4 14.8 %all-to-all-start = ((bf16[64,3,128]{2,1,0:T(4,128)(2,1)}), bf16[64,3,128]{2,1,0:T(4,128)(2,1)S(1)}, u32[]{:S(2)}, u32[]{:S(2)}) async-start(bf16[64,3,128]{2,1,0:T(4,128)(2,1)} %all_to_all.48), calls=%async_computation | async-start | bytes 131072 | tf_op jit(solution)/shard_map/all_to_all | solution.py:105
  23.3 5.0 %convert_reduce_fusion = (s32[64,64]{1,0:T(8,128)S(1)}, s32[64,64]{1,0:T(8,128)S(1)}, s32[64,64]{1,0:T(8,128)}, s32[64,64]{1,0:T(8,128)S(1)}, s32[64,64]{1,0:T(8,128)S(1)}, /*index=5*/s32[64,64]{1,0:T(8,128)S(1)}) fusion(s32[64,64]{1,0:T(8,128)S(1)} %get-tuple-element.39, pred[64,64]{1,0:T(8,128)(4,1)S(1)} %get-tuple-element.62, ...), kind=kLoop, calls=%fused_computation.1 | loop fusion | flops 6266880 | bytes 200704 | tf_op jit(solution)/shard_map/reduce_sum | solution.py:34
  28.4 1.8 fusion.40
  30.3 1.8 %fusion.46 = bf16[128,64,3]{0,2,1:T(4,128)(2,1)S(1)} fusion(s32[64,64]{1,0:T(8,128)S(1)} %get-tuple-element.61, pred[64,64]{1,0:T(8,128)(4,1)S(1)} %get-tuple-element.17, s32[64,64]{1,0:T(8,128)S(1)} %get-tuple-element.8), kind=kOutput, calls=%fused_computation.52 | convolution fusion | flops 4231168 | bytes 86016 | tf_op jit(solution)/shard_map/skq,skc->qsc/dot_general | solution.py:48
  33.0 1.8 fusion.52
  38.2 1.8 fusion.43
  40.0 2.9 %fusion.49 = bf16[128,64,3]{0,2,1:T(4,128)(2,1)S(1)} fusion(s32[64,64]{1,0:T(8,128)S(1)} %get-tuple-element.60, pred[64,64]{1,0:T(8,128)(4,1)} %get-tuple-element.43, s32[64,64]{1,0:T(8,128)} %get-tuple-element.7), kind=kOutput, calls=%fused_computation.53 | convolution fusion | flops 4231168 | bytes 86016 | tf_op jit(solution)/shard_map/skq,skc->qsc/dot_general | solution.py:48
  42.9 2.8 %fusion.55 = bf16[128,64,3]{0,2,1:T(4,128)(2,1)S(1)} fusion(s32[64,64]{1,0:T(8,128)} %get-tuple-element.37, pred[64,64]{1,0:T(8,128)(4,1)} %get-tuple-element.48, s32[64,64]{1,0:T(8,128)S(1)} %get-tuple-element.10), kind=kOutput, calls=%fused_computation.55 | convolution fusion | flops 4231168 | bytes 86016 | tf_op jit(solution)/shard_map/skq,skc->qsc/dot_general | solution.py:48
  46.3 3.2 %collective-permute-start = (bf16[192,128]{1,0:T(8,128)(2,1)S(1)}, bf16[192,128]{1,0:T(8,128)(2,1)S(1)}, u32[]{:S(2)}, u32[]{:S(2)}) collective-permute-start(bf16[192,128]{1,0:T(8,128)(2,1)S(1)} %all_to_all.50), channel_id=1, source_target_pairs={{0,64},{64,0},{128,192},{192,128},{256,320},{320,256},{384,448},{4... | collective-permute-start | bytes 147464 | tf_op jit(solution)/shard_map/ppermute | solution.py:10
  54.3 11.5 %all-to-all-start.1 = ((bf16[64,3,128]{2,1,0:T(4,128)(2,1)}), bf16[64,3,128]{2,1,0:T(4,128)(2,1)S(1)}, u32[]{:S(2)}, u32[]{:S(2)}) async-start(bf16[64,3,128]{2,1,0:T(4,128)(2,1)} %all_to_all.51), calls=%async_computation.1 | async-start | bytes 131072 | tf_op jit(solution)/shard_map/all_to_all | solution.py:105
  65.8 9.8 %all-to-all-done.1 = bf16[64,3,128]{2,1,0:T(4,128)(2,1)S(1)} async-done(((bf16[64,3,128]{2,1,0:T(4,128)(2,1)}), bf16[64,3,128]{2,1,0:T(4,128)(2,1)S(1)}, u32[]{:S(2)}, u32[]{:S(2)}) %all-to-all-start.1) | async-done | bytes 49184 | tf_op jit(solution)/shard_map/all_to_all | solution.py:105
  75.6 4.2 %collective-permute-start.1 = (bf16[192,128]{1,0:T(8,128)(2,1)S(1)}, bf16[192,128]{1,0:T(8,128)(2,1)S(1)}, u32[]{:S(2)}, u32[]{:S(2)}) collective-permute-start(bf16[192,128]{1,0:T(8,128)(2,1)S(1)} %all_to_all.53), channel_id=1, source_target_pairs={{0,128},{64,192},{128,0},{192,64},{256,384},{320,448},{384,256},{4... | collective-permute-start | bytes 147464 | tf_op jit(solution)/shard_map/ppermute | solution.py:10
  83.8 6.6 %all-to-all-start.2 = ((bf16[64,3,128]{2,1,0:T(4,128)(2,1)}), bf16[64,3,128]{2,1,0:T(4,128)(2,1)S(1)}, u32[]{:S(2)}, u32[]{:S(2)}) async-start(bf16[64,3,128]{2,1,0:T(4,128)(2,1)} %all_to_all.54), calls=%async_computation.2 | async-start | bytes 131072 | tf_op jit(solution)/shard_map/all_to_all | solution.py:105
  90.5 9.9 %all-to-all-done.2 = bf16[64,3,128]{2,1,0:T(4,128)(2,1)S(1)} async-done(((bf16[64,3,128]{2,1,0:T(4,128)(2,1)}), bf16[64,3,128]{2,1,0:T(4,128)(2,1)S(1)}, u32[]{:S(2)}, u32[]{:S(2)}) %all-to-all-start.2) | async-done | bytes 49184 | tf_op jit(solution)/shard_map/all_to_all | solution.py:105
  100.4 7.1 %collective-permute-start.2 = (bf16[192,128]{1,0:T(8,128)(2,1)S(1)}, bf16[192,128]{1,0:T(8,128)(2,1)S(1)}, u32[]{:S(2)}, u32[]{:S(2)}) collective-permute-start(bf16[192,128]{1,0:T(8,128)(2,1)S(1)} %all_to_all.56), channel_id=1, source_target_pairs={{0,256},{64,320},{128,384},{192,448},{256,0},{320,64},{384,128},{4... | collective-permute-start | bytes 147464 | tf_op jit(solution)/shard_map/ppermute | solution.py:10
  110.4 7.4 %collective-permute-start.3 = (bf16[192,128]{1,0:T(8,128)(2,1)S(1)}, bf16[192,128]{1,0:T(8,128)(2,1)S(1)}, u32[]{:S(2)}, u32[]{:S(2)}) collective-permute-start(bf16[192,128]{1,0:T(8,128)(2,1)S(1)} %convolution_convert_fusion.2), channel_id=1, source_target_pairs={{0,256},{64,320},{128,384},{192,448},{256,0},{320,64},{384,128},{4... | collective-permute-start | bytes 147464 | tf_op jit(solution)/shard_map/ppermute | solution.py:10
  120.1 6.6 %all-to-all-start.3 = ((bf16[64,3,128]{2,1,0:T(4,128)(2,1)}), bf16[64,3,128]{2,1,0:T(4,128)(2,1)S(1)}, u32[]{:S(2)}, u32[]{:S(2)}) async-start(bf16[64,3,128]{2,1,0:T(4,128)(2,1)} %all_to_all.57), calls=%async_computation.3 | async-start | bytes 131072 | tf_op jit(solution)/shard_map/all_to_all | solution.py:140
  126.7 9.9 %all-to-all-done.3 = bf16[64,3,128]{2,1,0:T(4,128)(2,1)S(1)} async-done(((bf16[64,3,128]{2,1,0:T(4,128)(2,1)}), bf16[64,3,128]{2,1,0:T(4,128)(2,1)S(1)}, u32[]{:S(2)}, u32[]{:S(2)}) %all-to-all-start.3) | async-done | bytes 49184 | tf_op jit(solution)/shard_map/all_to_all | solution.py:140
  137.7 4.6 %collective-permute-start.4 = (bf16[192,128]{1,0:T(8,128)(2,1)S(1)}, bf16[192,128]{1,0:T(8,128)(2,1)S(1)}, u32[]{:S(2)}, u32[]{:S(2)}) collective-permute-start(bf16[192,128]{1,0:T(8,128)(2,1)S(1)} %convolution_convert_fusion.1), channel_id=1, source_target_pairs={{0,128},{64,192},{128,0},{192,64},{256,384},{320,448},{384,256},{4... | collective-permute-start | bytes 147464 | tf_op jit(solution)/shard_map/ppermute | solution.py:10
  144.6 6.3 %all-to-all-start.4 = ((bf16[64,3,128]{2,1,0:T(4,128)(2,1)}), bf16[64,3,128]{2,1,0:T(4,128)(2,1)S(1)}, u32[]{:S(2)}, u32[]{:S(2)}) async-start(bf16[64,3,128]{2,1,0:T(4,128)(2,1)} %all_to_all.60), calls=%async_computation.4 | async-start | bytes 131072 | tf_op jit(solution)/shard_map/all_to_all | solution.py:140
  150.9 9.9 %all-to-all-done.4 = bf16[64,3,128]{2,1,0:T(4,128)(2,1)S(1)} async-done(((bf16[64,3,128]{2,1,0:T(4,128)(2,1)}), bf16[64,3,128]{2,1,0:T(4,128)(2,1)S(1)}, u32[]{:S(2)}, u32[]{:S(2)}) %all-to-all-start.4) | async-done | bytes 49184 | tf_op jit(solution)/shard_map/all_to_all | solution.py:140
  161.9 1.9 %collective-permute-start.5 = (bf16[192,128]{1,0:T(8,128)(2,1)S(1)}, bf16[192,128]{1,0:T(8,128)(2,1)S(1)}, u32[]{:S(2)}, u32[]{:S(2)}) collective-permute-start(bf16[192,128]{1,0:T(8,128)(2,1)S(1)} %convolution_convert_fusion), channel_id=1, source_target_pairs={{0,64},{64,0},{128,192},{192,128},{256,320},{320,256},{384,448},{4... | collective-permute-start | bytes 147464 | tf_op jit(solution)/shard_map/ppermute | solution.py:10
  163.9 2.9 %collective-permute-done.5 = bf16[192,128]{1,0:T(8,128)(2,1)S(1)} collective-permute-done((bf16[192,128]{1,0:T(8,128)(2,1)S(1)}, bf16[192,128]{1,0:T(8,128)(2,1)S(1)}, u32[]{:S(2)}, u32[]{:S(2)}) %collective-permute-start.5) | collective-permute-done | bytes 49184 | tf_op jit(solution)/shard_map/ppermute | solution.py:10
  167.0 14.8 %all_to_all.72 = bf16[64,3,128]{2,1,0:T(4,128)(2,1)S(1)} all-to-all(bf16[64,3,128]{2,1,0:T(4,128)(2,1)S(1)} %all_to_all.63), channel_id=1, replica_groups=mesh['leaf'=8,'blk'=64] {'blk'}, dimensions={0} | all-to-all | bytes 98304 | tf_op jit(solution)/shard_map/all_to_all | solution.py:140
  (128 shorter events, 30.4 us)
Async XLA Ops:
  0.0 22.3 %copy-start.4 = (bf16[1,1,4,512,32]{3,4,2,1,0:T(8,128)(2,1)S(1)}, bf16[1,1,4,512,32]{3,4,2,1,0:T(8,128)(2,1)}, u32[]{:S(2)}) copy-start(bf16[1,1,4,512,32]{3,4,2,1,0:T(8,128)(2,1)} %param.5) | copy-start | bytes 393220
  0.0 6.2 %copy-start.1 = (bf16[1,1,3,256,512]{4,3,2,1,0:T(8,128)(2,1)S(1)}, bf16[1,1,3,256,512]{4,3,2,1,0:T(8,128)(2,1)}, u32[]{:S(2)}) copy-start(bf16[1,1,3,256,512]{4,3,2,1,0:T(8,128)(2,1)} %param.7) | copy-start | bytes 2359300
  2.1 20.2 %copy-start.10 = (s32[64]{0:T(128)}, s32[64]{0:T(128)S(1)}, u32[]{:S(2)}) copy-start(s32[64]{0:T(128)S(1)} %fusion.209) | copy-start | bytes 772
  4.9 1.3 copy-start.6
  6.2 16.2 %copy-start.2 = (bf16[512,32]{0,1:T(8,128)(2,1)}, bf16[512,32]{0,1:T(8,128)(2,1)S(1)}, u32[]{:S(2)}) copy-start(bf16[512,32]{0,1:T(8,128)(2,1)S(1)} %fusion.64) | copy-start | bytes 98308
  7.4 38.9 %all-to-all-start = ((bf16[64,3,128]{2,1,0:T(4,128)(2,1)}), bf16[64,3,128]{2,1,0:T(4,128)(2,1)S(1)}, u32[]{:S(2)}, u32[]{:S(2)}) async-start(bf16[64,3,128]{2,1,0:T(4,128)(2,1)} %all_to_all.48), calls=%async_computation | async-start | bytes 131072 | tf_op jit(solution)/shard_map/all_to_all | solution.py:105
  40.0 11.5 %copy-start = (bf16[1,1,4,512,512]{4,3,2,1,0:T(8,128)(2,1)S(1)}, bf16[1,1,4,512,512]{4,3,2,1,0:T(8,128)(2,1)}, u32[]{:S(2)}) copy-start(bf16[1,1,4,512,512]{4,3,2,1,0:T(8,128)(2,1)} %param.6) | copy-start | bytes 6291460
  46.3 4.8 %collective-permute-start = (bf16[192,128]{1,0:T(8,128)(2,1)S(1)}, bf16[192,128]{1,0:T(8,128)(2,1)S(1)}, u32[]{:S(2)}, u32[]{:S(2)}) collective-permute-start(bf16[192,128]{1,0:T(8,128)(2,1)S(1)} %all_to_all.50), channel_id=1, source_target_pairs={{0,64},{64,0},{128,192},{192,128},{256,320},{320,256},{384,448},{4... | collective-permute-start | bytes 147464 | tf_op jit(solution)/shard_map/ppermute | solution.py:10
  54.3 21.3 %all-to-all-start.1 = ((bf16[64,3,128]{2,1,0:T(4,128)(2,1)}), bf16[64,3,128]{2,1,0:T(4,128)(2,1)S(1)}, u32[]{:S(2)}, u32[]{:S(2)}) async-start(bf16[64,3,128]{2,1,0:T(4,128)(2,1)} %all_to_all.51), calls=%async_computation.1 | async-start | bytes 131072 | tf_op jit(solution)/shard_map/all_to_all | solution.py:105
  75.6 5.7 %collective-permute-start.1 = (bf16[192,128]{1,0:T(8,128)(2,1)S(1)}, bf16[192,128]{1,0:T(8,128)(2,1)S(1)}, u32[]{:S(2)}, u32[]{:S(2)}) collective-permute-start(bf16[192,128]{1,0:T(8,128)(2,1)S(1)} %all_to_all.53), channel_id=1, source_target_pairs={{0,128},{64,192},{128,0},{192,64},{256,384},{320,448},{384,256},{4... | collective-permute-start | bytes 147464 | tf_op jit(solution)/shard_map/ppermute | solution.py:10
  81.9 54.7 %copy-start.9 = (s32[64]{0:T(128)S(1)}, s32[64]{0:T(128)}, u32[]{:S(2)}) copy-start(s32[64]{0:T(128)} %get-tuple-element.65) | copy-start | bytes 772
  83.8 16.6 %all-to-all-start.2 = ((bf16[64,3,128]{2,1,0:T(4,128)(2,1)}), bf16[64,3,128]{2,1,0:T(4,128)(2,1)S(1)}, u32[]{:S(2)}, u32[]{:S(2)}) async-start(bf16[64,3,128]{2,1,0:T(4,128)(2,1)} %all_to_all.54), calls=%async_computation.2 | async-start | bytes 131072 | tf_op jit(solution)/shard_map/all_to_all | solution.py:105
  100.4 8.8 %collective-permute-start.2 = (bf16[192,128]{1,0:T(8,128)(2,1)S(1)}, bf16[192,128]{1,0:T(8,128)(2,1)S(1)}, u32[]{:S(2)}, u32[]{:S(2)}) collective-permute-start(bf16[192,128]{1,0:T(8,128)(2,1)S(1)} %all_to_all.56), channel_id=1, source_target_pairs={{0,256},{64,320},{128,384},{192,448},{256,0},{320,64},{384,128},{4... | collective-permute-start | bytes 147464 | tf_op jit(solution)/shard_map/ppermute | solution.py:10
  109.5 51.3 %copy-start.8 = (s32[64]{0:T(128)S(1)}, s32[64]{0:T(128)}, u32[]{:S(2)}) copy-start(s32[64]{0:T(128)} %get-tuple-element.66) | copy-start | bytes 772
  109.6 51.6 %copy-start.5 = (f32[512]{0:T(512)S(1)}, f32[512]{0:T(512)}, u32[]{:S(2)}) copy-start(f32[512]{0:T(512)} %fusion.200) | copy-start | bytes 6148
  110.4 8.9 %collective-permute-start.3 = (bf16[192,128]{1,0:T(8,128)(2,1)S(1)}, bf16[192,128]{1,0:T(8,128)(2,1)S(1)}, u32[]{:S(2)}, u32[]{:S(2)}) collective-permute-start(bf16[192,128]{1,0:T(8,128)(2,1)S(1)} %convolution_convert_fusion.2), channel_id=1, source_target_pairs={{0,256},{64,320},{128,384},{192,448},{256,0},{320,64},{384,128},{4... | collective-permute-start | bytes 147464 | tf_op jit(solution)/shard_map/ppermute | solution.py:10
  120.1 16.5 %all-to-all-start.3 = ((bf16[64,3,128]{2,1,0:T(4,128)(2,1)}), bf16[64,3,128]{2,1,0:T(4,128)(2,1)S(1)}, u32[]{:S(2)}, u32[]{:S(2)}) async-start(bf16[64,3,128]{2,1,0:T(4,128)(2,1)} %all_to_all.57), calls=%async_computation.3 | async-start | bytes 131072 | tf_op jit(solution)/shard_map/all_to_all | solution.py:140
  136.9 44.9 %copy-start.11 = (s32[64]{0:T(128)S(1)}, s32[64]{0:T(128)}, u32[]{:S(2)}) copy-start(s32[64]{0:T(128)} %copy-done.10) | copy-start | bytes 772
  137.0 45.2 %copy-start.3 = (bf16[512,32]{0,1:T(8,128)(2,1)S(1)}, bf16[512,32]{0,1:T(8,128)(2,1)}, u32[]{:S(2)}) copy-start(bf16[512,32]{0,1:T(8,128)(2,1)} %copy-done.2) | copy-start | bytes 98308
  137.0 45.2 %copy-start.7 = (f32[512]{0:T(512)S(1)}, f32[512]{0:T(512)}, u32[]{:S(2)}) copy-start(f32[512]{0:T(512)} %copy-done.6) | copy-start | bytes 6148
  137.0 45.2 %copy-start.12 = (bf16[512]{0:T(512)(128)(2,1)S(1)}, bf16[512]{0:T(512)(128)(2,1)}, u32[]{:S(2)}) copy-start(bf16[512]{0:T(512)(128)(2,1)} %get-tuple-element.64) | copy-start | bytes 3076
  137.7 6.1 %collective-permute-start.4 = (bf16[192,128]{1,0:T(8,128)(2,1)S(1)}, bf16[192,128]{1,0:T(8,128)(2,1)S(1)}, u32[]{:S(2)}, u32[]{:S(2)}) collective-permute-start(bf16[192,128]{1,0:T(8,128)(2,1)S(1)} %convolution_convert_fusion.1), channel_id=1, source_target_pairs={{0,128},{64,192},{128,0},{192,64},{256,384},{320,448},{384,256},{4... | collective-permute-start | bytes 147464 | tf_op jit(solution)/shard_map/ppermute | solution.py:10
  144.6 16.2 %all-to-all-start.4 = ((bf16[64,3,128]{2,1,0:T(4,128)(2,1)}), bf16[64,3,128]{2,1,0:T(4,128)(2,1)S(1)}, u32[]{:S(2)}, u32[]{:S(2)}) async-start(bf16[64,3,128]{2,1,0:T(4,128)(2,1)} %all_to_all.60), calls=%async_computation.4 | async-start | bytes 131072 | tf_op jit(solution)/shard_map/all_to_all | solution.py:140
  161.9 4.8 %collective-permute-start.5 = (bf16[192,128]{1,0:T(8,128)(2,1)S(1)}, bf16[192,128]{1,0:T(8,128)(2,1)S(1)}, u32[]{:S(2)}, u32[]{:S(2)}) collective-permute-start(bf16[192,128]{1,0:T(8,128)(2,1)S(1)} %convolution_convert_fusion), channel_id=1, source_target_pairs={{0,64},{64,0},{128,192},{192,128},{256,320},{320,256},{384,448},{4... | collective-permute-start | bytes 147464 | tf_op jit(solution)/shard_map/ppermute | solution.py:10
where the time goes:
time: 184 us; the launch traced here: 183 us
  starting transfers between devices  74.3 us (40%)
  waiting for transfers between devices  49.4 us (27%)
  matrix products  21.7 us (12%)
  blocking collectives  14.8 us (8%)
  other arithmetic  10.2 us (6%)
  local copies, waits for them, and re-layouts  9.51 us (5%)
  between operations  3.33 us (2%)
    all_to_all x3, starting transfers between devices, shards(): lax.all_to_all(buffer, 'blk', split_axis=0, concat_axis=0, tiled=True)  33 us
    ppermute x6, starting transfers between devices, partner_2(): lax.ppermute(array, axis, [(i, i ^ 1 << distance) for i in range(lax.axis...  28.5 us
    all_to_all x2, waiting for transfers between devices, shards(): lax.all_to_all(merged, 'blk', split_axis=0, concat_axis=0, tiled=True)  19.8 us
    all_to_all x3, waiting for transfers between devices, shards(): lax.all_to_all(buffer, 'blk', split_axis=0, concat_axis=0, tiled=True)  19.7 us
    all_to_all x1, blocking collectives, shards(): lax.all_to_all(merged, 'blk', split_axis=0, concat_axis=0, tiled=True)  14.8 us
    dot_general x6, matrix products, receive_matrix(): layout = jnp.einsum('skq,skc->qsc', place_hot, rank_hot)  13 us
    all_to_all x2, starting transfers between devices, shards(): lax.all_to_all(merged, 'blk', split_axis=0, concat_axis=0, tiled=True)  12.9 us
    ppermute x6, waiting for transfers between devices, partner_2(): lax.ppermute(array, axis, [(i, i ^ 1 << distance) for i in range(lax.axis...  9.93 us
  transfers between devices with their start and end apart: 11, of which 10 were waited for; matrix products, arithmetic and copies ran while one was open for 12% of the time, Pallas kernels for 0%

commit v1 on v0

v1 whole, which is shorter than its diff:
```python
import functools

import jax
import jax.numpy as jnp
from jax import lax
from jax.experimental import pallas as pl
from jax.experimental.pallas import tpu as pltpu
from jax.sharding import PartitionSpec as P

BLOCK = 128
SLOTS = 4
MESH = pl.DeviceIdType.MESH
NN = (((1,), (0,)), ((), ()))
NT = (((1,), (1,)), ((), ()))
TN = (((0,), (0,)), ((), ()))


def dot(left, right, dims=NN):
    return lax.dot_general(left, right, dims, preferred_element_type=jnp.float32)


def iota(shape, axis):
    return lax.broadcasted_iota(jnp.int32, shape, axis)


def one_hot(condition):
    return condition.astype(jnp.float32).astype(jnp.bfloat16)


def peer_of(step, me, sizes):
    xs, zs, cores = sizes
    z_at, x_at, core_at = step // (xs * cores), step // cores % xs, step % cores
    z_off = zs // 2 + (z_at + 1) // 2 * (1 - 2 * (z_at % 2))
    x_off = xs // 2 + (x_at + 1) // 2 * (1 - 2 * (x_at % 2))
    x = (me // (zs * cores) + x_off) % xs
    z = (me // cores % zs + z_off) % zs
    core = (me % cores + cores - 1 - core_at) % cores
    return (x * zs + z) * cores + core


def kernel(
    sizes,
    b_hbm,
    inv_hbm,
    cpl_hbm,
    wid_ref,
    tgt_hbm,
    out_ref,
    b_ref,
    inv_ref,
    cpl_ref,
    tbl_ref,
    send_mat,
    back_mat,
    take_mat,
    piece_out,
    piece_in,
    slot_out,
    slot_in,
    load_sem,
    pair_send,
    pair_recv,
    slot_send,
    slot_recv,
):
    levels, cols, width = b_ref.shape
    rows = cpl_ref.shape[1]
    owners, pieces = tbl_ref.shape[2], tbl_ref.shape[3]
    lanes = rows // pieces * cols
    piece_rows = rows // pieces
    places = width // piece_rows
    leaf_bits = lax.axis_size("leaf").bit_length() - 1
    group, me = lax.axis_index("leaf"), lax.axis_index("blk")
    slot_rows = owners * SLOTS

    def partner_of(level):
        bit = 1 << level % leaf_bits
        return group + bit - 2 * bit * (group // bit % 2)

    loads = [pltpu.make_async_copy(b_hbm, b_ref, load_sem.at[0])]
    for level in range(levels - 1):
        for side, source in enumerate((group, partner_of(level))):
            loads.append(
                pltpu.make_async_copy(
                    tgt_hbm.at[level, source],
                    tbl_ref.at[level, side],
                    load_sem.at[1 + 2 * level + side],
                )
            )
    base = 2 * levels - 1
    inv_loads = [
        pltpu.make_async_copy(inv_hbm.at[n], inv_ref.at[n], load_sem.at[base + n])
        for n in range(levels)
    ]
    cpl_loads = [
        pltpu.make_async_copy(cpl_hbm.at[n], cpl_ref.at[n], load_sem.at[base + levels + n])
        for n in range(levels - 1)
    ]
    loads[0].start()
    inv_loads[0].start()
    cpl_loads[0].start()
    for copy in loads[1:]:
        copy.start()
    for copy in inv_loads[1:] + cpl_loads[1:]:
        copy.start()

    barrier = pltpu.get_barrier_semaphore()

    def greet(step, carry):
        pl.semaphore_signal(
            barrier, inc=1, device_id=(group, peer_of(step, me, sizes)), device_id_type=MESH
        )
        return carry

    lax.fori_loop(0, owners - 1, greet, 0)
    for level in range(levels - 1):
        pl.semaphore_signal(barrier, inc=1, device_id=(partner_of(level), me), device_id_type=MESH)

    before = one_hot(iota((2 * pieces, 2 * pieces), 0) < iota((2 * pieces, 2 * pieces), 1))
    gather_rows = one_hot(iota((pieces, rows), 1) // piece_rows == iota((pieces, rows), 0))
    repeat = one_hot(iota((slot_rows, owners), 0) // SLOTS == iota((slot_rows, owners), 1))
    slot_rank = (iota((slot_rows, 2 * pieces), 0) % SLOTS).astype(jnp.float32)
    on_pair = iota((1, 2 * pieces), 1) // pieces

    def row_mask(level):
        return (iota((1, width), 1) < wid_ref[0, level] * BLOCK).astype(jnp.float32)

    def codes(own, pair):
        code = jnp.concatenate([own, pair], axis=1)
        ok = code // (owners * places) == on_pair
        return ok, code // places % owners, code % places

    def make_send(level):
        mine = tbl_ref[level, 0, pl.ds(me, 1), :]
        pair = tbl_ref[level, 1, pl.ds(me, 1), :]
        ok, dest, _ = codes(mine, pair)
        dest = jnp.where(ok, dest, -1)
        hit = (iota((slot_rows, 2 * pieces), 0) // SLOTS == dest).astype(jnp.float32)
        count = dot(hit.astype(jnp.bfloat16), before)
        chosen = jnp.where(count == slot_rank, hit, 0.0).astype(jnp.bfloat16)
        send_mat[level] = chosen

    def make_back(level):
        back_mat[level] = jnp.transpose(send_mat[level].astype(jnp.float32)).astype(jnp.bfloat16)

    def make_take(level):
        ok, dest, place = codes(tbl_ref[level, 0], tbl_ref[level, 1])
        match = (ok & (dest == me)).astype(jnp.float32)
        spot = dot(repeat, (match * (place + 1).astype(jnp.float32)).astype(jnp.bfloat16))
        hit = dot(repeat, match.astype(jnp.bfloat16))
        count = dot(hit.astype(jnp.bfloat16), before)
        spot = jnp.sum(jnp.where(count == slot_rank, spot, 0.0), axis=1, keepdims=True)
        at = (iota((1, width), 1) // piece_rows + 1).astype(jnp.float32)
        take_mat[level] = one_hot(spot == at)

    def spread(value):
        turn = iota(value.shape, 1) % piece_rows
        return jnp.concatenate(
            [jnp.where(turn == i, value, 0.0) for i in range(piece_rows)], axis=0
        ).astype(jnp.bfloat16)

    def collect(value):
        turn = iota((cols, value.shape[1]), 1) % piece_rows
        out = value[:cols]
        for i in range(1, piece_rows):
            out = jnp.where(turn == i, value[i * cols : (i + 1) * cols], out)
        return out

    def pair_copy(phase, level):
        return pltpu.make_async_remote_copy(
            src_ref=piece_out.at[phase],
            dst_ref=piece_in.at[phase],
            send_sem=pair_send.at[phase],
            recv_sem=pair_recv.at[phase],
            device_id=(partner_of(level), me),
            device_id_type=MESH,
        )

    def send_slots(phase, value):
        slot_out[phase] = value.reshape(owners, SLOTS, lanes)

        def send(step, carry):
            peer = peer_of(step, me, sizes)
            pltpu.make_async_remote_copy(
                src_ref=slot_out.at[phase, peer],
                dst_ref=slot_in.at[phase, me],
                send_sem=slot_send.at[phase],
                recv_sem=slot_recv.at[phase],
                device_id=(group, peer),
                device_id_type=MESH,
            ).start()
            return carry

        lax.fori_loop(0, owners - 1, send, 0)
        pltpu.make_async_copy(
            slot_out.at[phase, me], slot_in.at[phase, me], slot_recv.at[phase]
        ).start()

    def slots_arrived(phase):
        pltpu.make_async_copy(slot_out.at[phase], slot_in.at[phase], slot_recv.at[phase]).wait()
        return slot_in[phase].reshape(slot_rows, lanes)

    forward = []
    for level in range(levels):
        if level == 0:
            loads[0].wait()
            residual = b_ref[0]
            inv_loads[0].wait()
        solved = row_mask(level) * dot(residual, inv_ref[level], NT)
        solved = solved.astype(jnp.bfloat16)
        forward.append(solved)
        if level + 1 == levels:
            break
        if level == 0:
            cpl_loads[0].wait()
        blocks = dot(solved, cpl_ref[level], NT)
        own = dot(gather_rows, spread(blocks), NT).astype(jnp.bfloat16)
        piece_out[level] = own
        if level == 0:
            pl.semaphore_wait(barrier, owners - 1 + levels - 1)
        copy = pair_copy(level, level)
        copy.start()
        if level == 0:
            for load in loads[1:]:
                load.wait()
            make_send(0)
        copy.wait_recv()
        both = jnp.concatenate([own, piece_in[level]], axis=0)
        send_slots(level, dot(send_mat[level], both).astype(jnp.bfloat16))
        make_take(level)
        if level == 0:
            for load in inv_loads[1:] + cpl_loads[1:]:
                load.wait()
        if level + 2 < levels:
            make_send(level + 1)
        make_back(level)
        arrived = slots_arrived(level)
        incoming = collect(dot(arrived, take_mat[level], TN))
        residual = (b_ref[level + 1].astype(jnp.float32) - incoming).astype(jnp.bfloat16)

    above = None
    for level in reversed(range(levels)):
        if level + 1 == levels:
            back_side = forward[level].astype(jnp.float32)
        else:
            phase = levels - 1 + level
            reply = dot(take_mat[level], spread(above), NT).astype(jnp.bfloat16)
            send_slots(phase, reply)
            arrived = slots_arrived(phase)
            both = dot(back_mat[level], arrived)
            piece_out[phase] = both[pieces:].astype(jnp.bfloat16)
            copy = pair_copy(phase, level)
            copy.start()
            copy.wait_recv()
            gathered = (both[:pieces] + piece_in[phase].astype(jnp.float32)).astype(jnp.bfloat16)
            rows_in = collect(dot(gathered, gather_rows, TN)).astype(jnp.bfloat16)
            back_side = forward[level].astype(jnp.float32) - dot(rows_in, cpl_ref[level])
            back_side = back_side.astype(jnp.bfloat16).astype(jnp.float32)
        masked = (row_mask(level) * back_side).astype(jnp.bfloat16)
        answer = (row_mask(level) * dot(masked, inv_ref[level])).astype(jnp.bfloat16)
        out_ref[level] = answer
        above = answer.astype(jnp.float32)

    for phase in range(2 * (levels - 1)):
        pair_copy(phase, phase % (levels - 1)).wait_send()
        pltpu.make_async_copy(
            slot_out.at[phase, pl.ds(0, owners - 1)],
            slot_in.at[phase, pl.ds(0, owners - 1)],
            slot_send.at[phase],
        ).wait()


def shards(right_sides, inverses, couplings, widths, targets):
    owners = lax.axis_size("blk")
    right = jnp.swapaxes(right_sides[0, 0], 1, 2)
    inverse, coupling = inverses[0, 0], couplings[0, 0]
    levels, cols, width = right.shape
    rows, pieces = coupling.shape[1], targets.shape[3]
    lanes = rows // pieces * cols
    phases = 2 * (levels - 1)
    slot_rows = owners * SLOTS
    hbm = pl.BlockSpec(memory_space=pl.ANY)
    out = pl.pallas_call(
        functools.partial(kernel, (4, 8, 2)),
        out_shape=jax.ShapeDtypeStruct((levels, cols, width), jnp.bfloat16),
        in_specs=[hbm, hbm, hbm, pl.BlockSpec(memory_space=pltpu.SMEM), hbm],
        out_specs=pl.BlockSpec(memory_space=pltpu.VMEM),
        scratch_shapes=[
            pltpu.VMEM((levels, cols, width), jnp.bfloat16),
            pltpu.VMEM((levels, width, width), jnp.bfloat16),
            pltpu.VMEM((levels - 1, rows, width), jnp.bfloat16),
            pltpu.VMEM((levels - 1, 2, owners, pieces), jnp.int32),
            pltpu.VMEM((levels - 1, slot_rows, 2 * pieces), jnp.bfloat16),
            pltpu.VMEM((levels - 1, 2 * pieces, slot_rows), jnp.bfloat16),
            pltpu.VMEM((levels - 1, slot_rows, width), jnp.bfloat16),
            pltpu.VMEM((phases, pieces, lanes), jnp.bfloat16),
            pltpu.VMEM((phases, pieces, lanes), jnp.bfloat16),
            pltpu.VMEM((phases, owners, SLOTS, lanes), jnp.bfloat16),
            pltpu.VMEM((phases, owners, SLOTS, lanes), jnp.bfloat16),
            pltpu.SemaphoreType.DMA((4 * levels - 2,)),
            pltpu.SemaphoreType.DMA((phases,)),
            pltpu.SemaphoreType.DMA((phases,)),
            pltpu.SemaphoreType.DMA((phases,)),
            pltpu.SemaphoreType.DMA((phases,)),
        ],
        compiler_params=pltpu.CompilerParams(collective_id=0, has_side_effects=True),
    )(right, inverse, coupling, widths[0], targets)
    return jnp.swapaxes(out, 1, 2)[None, None]


def solution(mesh):
    return jax.shard_map(
        shards,
        mesh=mesh,
        in_specs=(
            P("leaf", "blk", None, None, None),
            P("leaf", "blk", None, None, None),
            P("leaf", "blk", None, None, None),
            P("leaf", "blk", None),
            P(),
        ),
        out_specs=P("leaf", "blk", None, None, None),
        check_vma=False,
    )
```

time: 184 us -> 86.8 us (0.47)
  Pallas kernels: 0 us -> 85.1 us
  starting transfers between devices: 74.3 us -> 0 us
  waiting for transfers between devices: 49.4 us -> 0 us
  matrix products: 21.7 us -> 0 us
  blocking collectives: 14.8 us -> 0 us
  other arithmetic: 10.2 us -> 0 us
  local copies, waits for them, and re-layouts: 9.51 us -> 1.57 us
  between operations: 3.33 us -> 0.01 us
    pallas_call x0 -> x1, Pallas kernels: none -> 85.1 us  [shards(): pl.pallas_call(functools.partial(kernel, (4, 8, 2)), out_shape=jax.ShapeD...]
    all_to_all x5 -> x0, starting transfers between devices: 45.9 us -> none  [the longest x3 33 us: shards(): lax.all_to_all(buffer, 'blk', split_axis=0, concat_axis=0, tiled=True)]
    all_to_all x5 -> x0, waiting for transfers between devices: 39.4 us -> none  [the longest x2 19.8 us: shards(): lax.all_to_all(merged, 'blk', split_axis=0, concat_axis=0, tiled=True)]
    ppermute x6 -> x0, starting transfers between devices: 28.5 us -> none  [partner_2(): lax.ppermute(array, axis, [(i, i ^ 1 << distance) for i in range(lax.axis...]
    dot_general x34 -> x0, matrix products: 21.7 us -> none  [the longest x6 13 us: receive_matrix(): layout = jnp.einsum('skq,skc->qsc', place_hot, rank_hot)]
    all_to_all x1 -> x0, blocking collectives: 14.8 us -> none  [shards(): lax.all_to_all(merged, 'blk', split_axis=0, concat_axis=0, tiled=True)]
    ppermute x6 -> x0, waiting for transfers between devices: 9.93 us -> none  [partner_2(): lax.ppermute(array, axis, [(i, i ^ 1 << distance) for i in range(lax.axis...]
    reduce_sum x4 -> x0, other arithmetic: 5.33 us -> none  [rank_pieces(): return jnp.sum(matches.astype(jnp.int32), axis=-2)]
  transfers between devices with their start and end apart: 11 -> 0, of which waited for: 10 -> 0; matrix products, arithmetic and copies ran while one was open for 12% -> 0% of each run, Pallas kernels for 0% -> 0%
where the time goes in v1:
time: 86.8 us; the launch traced here: 86.6 us
  Pallas kernels  85.1 us (98%)
  local copies, waits for them, and re-layouts  1.57 us (2%)
    pallas_call x1, Pallas kernels, shards(): pl.pallas_call(functools.partial(kernel, (4, 8, 2)), out_shape=jax.ShapeD...  85.1 us

profile of v1, /device:TPU:1, one launch (start us, length us, event | category | flops | bytes accessed | tf_op | source)
XLA Modules:
  0.0 86.6 jit_solution(16812991795545637240)
XLA Ops:
  0.0 85.1 %shard_map.55 = bf16[4,32,512]{2,1,0:T(8,128)(2,1)} custom-call(bf16[4,32,512]{2,1,0:T(8,128)(2,1)} %bitcast.12, bf16[4,512,512]{2,1,0:T(8,128)(2,1)} %bitcast.9, bf16[3,256,512]{2,1,0:T(8,128)(2,1)} %bitcast.10, s32[1,4]{1,0:T(1,128)} %bitcast.13, s32[3,8,64,64]{3,2,1,0:T(8,128)} %tgt_hbm.1), custom_call_target="tpu_custom_call" | custom-call | tf_op jit(solution)/shard_map/pallas_call | solution.py:283
  85.1 1.6 %copy.7 = bf16[1,1,4,512,32]{3,4,2,1,0:T(8,128)(2,1)} copy(bf16[1,1,4,512,32]{3,4,2,1,0:T(8,128)(2,1)} %bitcast.11) | data formatting | bytes 262144

commit v2 on v1

v2 whole, which is shorter than its diff:
```python
import functools

import jax
import jax.numpy as jnp
from jax import lax
from jax.experimental import pallas as pl
from jax.experimental.pallas import tpu as pltpu
from jax.sharding import PartitionSpec as P

BLOCK = 128
SLOTS = 4
MESH = pl.DeviceIdType.MESH
NN = (((1,), (0,)), ((), ()))
NT = (((1,), (1,)), ((), ()))
TN = (((0,), (0,)), ((), ()))


def dot(left, right, dims=NN):
    return lax.dot_general(left, right, dims, preferred_element_type=jnp.float32)


def iota(shape, axis):
    return lax.broadcasted_iota(jnp.int32, shape, axis)


def one_hot(condition):
    return condition.astype(jnp.float32).astype(jnp.bfloat16)


def each_owner(me, sizes, visit):
    xs, zs, cores = sizes
    z, core = lax.rem(lax.div(me, cores), zs), lax.rem(me, cores)
    x = lax.div(me, zs * cores)
    x_order = sorted(range(xs), key=lambda off: -min(off, xs - off))
    columns = [
        lax.rem(x + off, xs) * (zs * cores) + lax.rem(core + 1 + n, cores)
        for off in x_order
        for n in range(cores)
    ]

    def plane(step, carry):
        off = zs // 2 + lax.div(step + 1, 2) * (1 - 2 * lax.rem(step, 2))
        row = lax.rem(z + off, zs) * cores
        for column in columns:
            visit(column + row, False)
        return carry

    lax.fori_loop(0, zs - 1, plane, 0)
    for column in columns[:-1]:
        visit(column + z * cores, False)
    visit(me, True)


def kernel(
    sizes,
    b_hbm,
    inv_hbm,
    cpl_hbm,
    wid_ref,
    tgt_hbm,
    out_ref,
    b_ref,
    inv_ref,
    cpl_ref,
    tbl_ref,
    send_mat,
    take_mat,
    slot_out,
    slot_in,
    load_sem,
    slot_send,
    slot_recv,
    near_sem,
):
    levels, cols, width = b_ref.shape
    rows = cpl_ref.shape[1]
    owners, pieces = tbl_ref.shape[2], tbl_ref.shape[3]
    lanes = rows // pieces * cols
    piece_rows = rows // pieces
    places = width // piece_rows
    leaf_bits = lax.axis_size("leaf").bit_length() - 1
    group, me = lax.axis_index("leaf"), lax.axis_index("blk")
    slot_rows = 2 * owners * SLOTS

    def partner_of(level):
        bit = 1 << level % leaf_bits
        return group + bit - 2 * bit * (group // bit % 2)

    loads = [pltpu.make_async_copy(b_hbm, b_ref, load_sem.at[0])]
    for level in range(levels - 1):
        for side, source in enumerate((group, partner_of(level))):
            loads.append(
                pltpu.make_async_copy(
                    tgt_hbm.at[level, source],
                    tbl_ref.at[level, side],
                    load_sem.at[1 + 2 * level + side],
                )
            )
    base = 2 * levels - 1
    inv_loads = [
        pltpu.make_async_copy(inv_hbm.at[n], inv_ref.at[n], load_sem.at[base + n])
        for n in range(levels)
    ]
    cpl_loads = [
        pltpu.make_async_copy(cpl_hbm.at[n], cpl_ref.at[n], load_sem.at[base + levels + n])
        for n in range(levels - 1)
    ]
    loads[1].start()
    loads[0].start()
    inv_loads[0].start()
    cpl_loads[0].start()
    for copy in loads[2:] + inv_loads[1:] + cpl_loads[1:]:
        copy.start()

    barrier = pltpu.get_barrier_semaphore()

    def signal(semaphore, leaf, blk):
        pl.semaphore_signal(semaphore, inc=1, device_id=(leaf, blk), device_id_type=MESH)

    def greet(owner, last):
        if not last:
            signal(barrier, group, owner)

    each_owner(me, sizes, greet)
    for level in range(levels - 1):
        signal(barrier, partner_of(level), me)

    before = one_hot(iota((pieces, pieces), 0) < iota((pieces, pieces), 1))
    widen = one_hot(iota((pieces, rows), 1) // piece_rows == iota((pieces, rows), 0))
    repeat = one_hot(iota((slot_rows, 2 * owners), 0) // SLOTS == iota((slot_rows, 2 * owners), 1))
    slot_rank = (iota((slot_rows, pieces), 0) % SLOTS).astype(jnp.float32)

    def row_mask(level):
        return (iota((1, width), 1) < wid_ref[0, level] * BLOCK).astype(jnp.float32)

    def make_send(level):
        dest = tbl_ref[level, 0, pl.ds(me, 1), :] // places
        hit = (iota((slot_rows, pieces), 0) // SLOTS == dest).astype(jnp.float32)
        count = dot(hit.astype(jnp.bfloat16), before)
        chosen = jnp.where(count == slot_rank, hit, 0.0).astype(jnp.bfloat16)
        send_mat[level] = dot(chosen, widen).astype(jnp.bfloat16)

    def make_take(level):
        code = jnp.concatenate([tbl_ref[level, 0], tbl_ref[level, 1]], axis=0)
        wanted = iota((2 * owners, 1), 0) // owners * owners + me
        match = (code // places == wanted).astype(jnp.float32)
        spot = dot(repeat, (match * (code % places + 1).astype(jnp.float32)).astype(jnp.bfloat16))
        hit = dot(repeat, match.astype(jnp.bfloat16))
        count = dot(hit.astype(jnp.bfloat16), before)
        spot = jnp.sum(jnp.where(count == slot_rank, spot, 0.0), axis=1, keepdims=True)
        at = (iota((1, width), 1) // piece_rows + 1).astype(jnp.float32)
        take_mat[level] = one_hot(spot == at)

    def spread(value):
        turn = iota(value.shape, 1) % piece_rows
        return jnp.concatenate(
            [jnp.where(turn == i, value, 0.0) for i in range(piece_rows)], axis=0
        ).astype(jnp.bfloat16)

    def collect(value):
        turn = iota((cols, value.shape[1]), 1) % piece_rows
        out = value[:cols]
        for i in range(1, piece_rows):
            out = jnp.where(turn == i, value[i * cols : (i + 1) * cols], out)
        return out

    def send_slots(phase, level, value):
        slot_out[phase] = value.astype(jnp.bfloat16).reshape(2, owners, SLOTS, lanes)
        partner = partner_of(level)

        def send(owner, last):
            for side in (1, 0):
                if side == 0 and last:
                    pltpu.make_async_copy(
                        slot_out.at[phase, 0, me], slot_in.at[phase, 0, me], slot_recv.at[phase]
                    ).start()
                    continue
                pltpu.make_async_remote_copy(
                    src_ref=slot_out.at[phase, side, owner],
                    dst_ref=slot_in.at[phase, side, me],
                    send_sem=slot_send.at[phase],
                    recv_sem=slot_recv.at[phase],
                    device_id=(partner if side else group, owner),
                    device_id_type=MESH,
                ).start()

        each_owner(me, sizes, send)

    def slots_arrived(phase):
        pltpu.make_async_copy(slot_out.at[phase], slot_in.at[phase], slot_recv.at[phase]).wait()
        return slot_in[phase].reshape(slot_rows, lanes)

    forward = []
    for level in range(levels):
        if level == 0:
            loads[1].wait()
            make_send(0)
            loads[0].wait()
            residual = b_ref[0]
            inv_loads[0].wait()
        solved = row_mask(level) * dot(residual, inv_ref[level], NT)
        solved = solved.astype(jnp.bfloat16)
        forward.append(solved)
        if level + 1 == levels:
            break
        if level == 0:
            cpl_loads[0].wait()
        blocks = dot(solved, cpl_ref[level], NT)
        buffer = dot(send_mat[level], spread(blocks), NT)
        if level == 0:
            pl.semaphore_wait(barrier, owners - 1 + levels - 1)
            signal(near_sem, partner_of(0), me)
            pl.semaphore_wait(near_sem, 1)
        send_slots(level, level, buffer)
        if level == 0:
            for load in loads[2:] + inv_loads[1:] + cpl_loads[1:]:
                load.wait()
        make_take(level)
        if level + 2 < levels:
            make_send(level + 1)
        arrived = slots_arrived(level)
        incoming = collect(dot(arrived, take_mat[level], TN))
        residual = (b_ref[level + 1].astype(jnp.float32) - incoming).astype(jnp.bfloat16)

    above = None
    for level in reversed(range(levels)):
        if level + 1 == levels:
            back_side = forward[level].astype(jnp.float32)
        else:
            phase = levels - 1 + level
            send_slots(phase, level, dot(take_mat[level], spread(above), NT))
            arrived = slots_arrived(phase)
            rows_in = collect(dot(arrived, send_mat[level], TN)).astype(jnp.bfloat16)
            back_side = forward[level].astype(jnp.float32) - dot(rows_in, cpl_ref[level])
            back_side = back_side.astype(jnp.bfloat16).astype(jnp.float32)
        masked = (row_mask(level) * back_side).astype(jnp.bfloat16)
        answer = (row_mask(level) * dot(masked, inv_ref[level])).astype(jnp.bfloat16)
        out_ref[level] = answer
        above = answer.astype(jnp.float32)

    for phase in range(2 * (levels - 1)):
        for side, count in ((0, owners - 1), (1, owners)):
            pltpu.make_async_copy(
                slot_out.at[phase, side, pl.ds(0, count)],
                slot_in.at[phase, side, pl.ds(0, count)],
                slot_send.at[phase],
            ).wait()


def shards(right_sides, inverses, couplings, widths, targets):
    owners = lax.axis_size("blk")
    right = jnp.swapaxes(right_sides[0, 0], 1, 2)
    inverse, coupling = inverses[0, 0], couplings[0, 0]
    levels, cols, width = right.shape
    rows, pieces = coupling.shape[1], targets.shape[3]
    lanes = rows // pieces * cols
    phases = 2 * (levels - 1)
    slot_rows = 2 * owners * SLOTS
    hbm = pl.BlockSpec(memory_space=pl.ANY)
    out = pl.pallas_call(
        functools.partial(kernel, (4, 8, 2)),
        out_shape=jax.ShapeDtypeStruct((levels, cols, width), jnp.bfloat16),
        in_specs=[hbm, hbm, hbm, pl.BlockSpec(memory_space=pltpu.SMEM), hbm],
        out_specs=pl.BlockSpec(memory_space=pltpu.VMEM),
        scratch_shapes=[
            pltpu.VMEM((levels, cols, width), jnp.bfloat16),
            pltpu.VMEM((levels, width, width), jnp.bfloat16),
            pltpu.VMEM((levels - 1, rows, width), jnp.bfloat16),
            pltpu.VMEM((levels - 1, 2, owners, pieces), jnp.int32),
            pltpu.VMEM((levels - 1, slot_rows, rows), jnp.bfloat16),
            pltpu.VMEM((levels - 1, slot_rows, width), jnp.bfloat16),
            pltpu.VMEM((phases, 2, owners, SLOTS, lanes), jnp.bfloat16),
            pltpu.VMEM((phases, 2, owners, SLOTS, lanes), jnp.bfloat16),
            pltpu.SemaphoreType.DMA((4 * levels - 2,)),
            pltpu.SemaphoreType.DMA((phases,)),
            pltpu.SemaphoreType.DMA((phases,)),
            pltpu.SemaphoreType.REGULAR,
        ],
        compiler_params=pltpu.CompilerParams(collective_id=0, has_side_effects=True),
    )(right, inverse, coupling, widths[0], targets)
    return jnp.swapaxes(out, 1, 2)[None, None]


def solution(mesh):
    return jax.shard_map(
        shards,
        mesh=mesh,
        in_specs=(
            P("leaf", "blk", None, None, None),
            P("leaf", "blk", None, None, None),
            P("leaf", "blk", None, None, None),
            P("leaf", "blk", None),
            P(),
        ),
        out_specs=P("leaf", "blk", None, None, None),
        check_vma=False,
    )
```

time: 86.8 us -> 70.8 us (0.82)
  Pallas kernels: 85.1 us -> 69.1 us
    pallas_call x1, Pallas kernels: 85.1 us -> 69.1 us  [shards(): pl.pallas_call(functools.partial(kernel, (4, 8, 2)), out_shape=jax.ShapeD...]
where the time goes in v2:
time: 70.8 us; the launch traced here: 70.7 us
  Pallas kernels  69.1 us (98%)
  local copies, waits for them, and re-layouts  1.57 us (2%)
    pallas_call x1, Pallas kernels, shards(): pl.pallas_call(functools.partial(kernel, (4, 8, 2)), out_shape=jax.ShapeD...  69.1 us
    unnamed x1, local copies, waits for them, and re-layouts  1.57 us

profile of v2, /device:TPU:1, one launch (start us, length us, event | category | flops | bytes accessed | tf_op | source)
XLA Modules:
  0.0 70.7 jit_solution(9245608976221216681)
XLA Ops:
  0.0 69.1 %shard_map.55 = bf16[4,32,512]{2,1,0:T(8,128)(2,1)} custom-call(bf16[4,32,512]{2,1,0:T(8,128)(2,1)} %bitcast.12, bf16[4,512,512]{2,1,0:T(8,128)(2,1)} %bitcast.9, bf16[3,256,512]{2,1,0:T(8,128)(2,1)} %bitcast.10, s32[1,4]{1,0:T(1,128)} %bitcast.13, s32[3,8,64,64]{3,2,1,0:T(8,128)} %tgt_hbm.1), custom_call_target="tpu_custom_call" | custom-call | tf_op jit(solution)/shard_map/pallas_call | solution.py:260
  69.1 1.6 %copy.7 = bf16[1,1,4,512,32]{3,4,2,1,0:T(8,128)(2,1)} copy(bf16[1,1,4,512,32]{3,4,2,1,0:T(8,128)(2,1)} %bitcast.11) | data formatting | bytes 262144

commit v3 on v2

--- a/solution.py
+++ b/solution.py
@@ -56,15 +56,18 @@
     b_hbm,
     inv_hbm,
     cpl_hbm,
-    wid_ref,
+    wid_hbm,
     tgt_hbm,
     out_ref,
+    wid_ref,
     b_ref,
     inv_ref,
     cpl_ref,
     tbl_ref,
     send_mat,
     take_mat,
+    fold_ref,
+    base_ref,
     slot_out,
     slot_in,
     load_sem,
@@ -105,8 +108,10 @@
         pltpu.make_async_copy(cpl_hbm.at[n], cpl_ref.at[n], load_sem.at[base + levels + n])
         for n in range(levels - 1)
     ]
+    wid_load = pltpu.make_async_copy(wid_hbm, wid_ref, load_sem.at[base + 2 * levels - 1])
     loads[1].start()
     loads[0].start()
+    wid_load.start()
     inv_loads[0].start()
     cpl_loads[0].start()
     for copy in loads[2:] + inv_loads[1:] + cpl_loads[1:]:
@@ -121,9 +126,9 @@
         if not last:
             signal(barrier, group, owner)
 
-    each_owner(me, sizes, greet)
     for level in range(levels - 1):
         signal(barrier, partner_of(level), me)
+    each_owner(me, sizes, greet)
 
     before = one_hot(iota((pieces, pieces), 0) < iota((pieces, pieces), 1))
     widen = one_hot(iota((pieces, rows), 1) // piece_rows == iota((pieces, rows), 0))
@@ -190,22 +195,27 @@
         pltpu.make_async_copy(slot_out.at[phase], slot_in.at[phase], slot_recv.at[phase]).wait()
         return slot_in[phase].reshape(slot_rows, lanes)
 
-    forward = []
-    for level in range(levels):
-        if level == 0:
-            loads[1].wait()
-            make_send(0)
-            loads[0].wait()
-            residual = b_ref[0]
-            inv_loads[0].wait()
-        solved = row_mask(level) * dot(residual, inv_ref[level], NT)
-        solved = solved.astype(jnp.bfloat16)
-        forward.append(solved)
-        if level + 1 == levels:
-            break
-        if level == 0:
-            cpl_loads[0].wait()
-        blocks = dot(solved, cpl_ref[level], NT)
+    def fold(level):
+        live = (cpl_ref[level].astype(jnp.float32) * row_mask(level)).astype(jnp.bfloat16)
+        fold_ref[level] = dot(live, inv_ref[level]).astype(jnp.bfloat16)
+
+    def forward_of(level, residual):
+        return (row_mask(level) * dot(residual, inv_ref[level], NT)).astype(jnp.bfloat16)
+
+    def settled(level, forward):
+        return dot(forward, inv_ref[level])
+
+    top = levels - 1
+    loads[1].wait()
+    make_send(0)
+    loads[0].wait()
+    inv_loads[0].wait()
+    wid_load.wait()
+    solved = forward_of(0, b_ref[0])
+    cpl_loads[0].wait()
+    blocks = dot(solved, cpl_ref[0], NT)
+    base_ref[0] = settled(0, solved)
+    for level in range(top):
         buffer = dot(send_mat[level], spread(blocks), NT)
         if level == 0:
             pl.semaphore_wait(barrier, owners - 1 + levels - 1)
@@ -215,28 +225,29 @@
         if level == 0:
             for load in loads[2:] + inv_loads[1:] + cpl_loads[1:]:
                 load.wait()
+            fold(0)
+        else:
+            base_ref[level] = settled(level, forward_of(level, residual))
         make_take(level)
-        if level + 2 < levels:
+        if level + 1 < top:
             make_send(level + 1)
+            fold(level + 1)
         arrived = slots_arrived(level)
         incoming = collect(dot(arrived, take_mat[level], TN))
         residual = (b_ref[level + 1].astype(jnp.float32) - incoming).astype(jnp.bfloat16)
-
-    above = None
-    for level in reversed(range(levels)):
-        if level + 1 == levels:
-            back_side = forward[level].astype(jnp.float32)
-        else:
-            phase = levels - 1 + level
-            send_slots(phase, level, dot(take_mat[level], spread(above), NT))
-            arrived = slots_arrived(phase)
-            rows_in = collect(dot(arrived, send_mat[level], TN)).astype(jnp.bfloat16)
-            back_side = forward[level].astype(jnp.float32) - dot(rows_in, cpl_ref[level])
-            back_side = back_side.astype(jnp.bfloat16).astype(jnp.float32)
-        masked = (row_mask(level) * back_side).astype(jnp.bfloat16)
-        answer = (row_mask(level) * dot(masked, inv_ref[level])).astype(jnp.bfloat16)
-        out_ref[level] = answer
-        above = answer.astype(jnp.float32)
+        if level + 1 < top:
+            blocks = dot(residual, fold_ref[level + 1], NT)
+
+    above = row_mask(top) * settled(top, forward_of(top, residual))
+    for level in reversed(range(top)):
+        phase = top + level
+        above = above.astype(jnp.bfloat16)
+        out_ref[level + 1] = above
+        send_slots(phase, level, dot(take_mat[level], spread(above.astype(jnp.float32)), NT))
+        arrived = slots_arrived(phase)
+        rows_in = collect(dot(arrived, send_mat[level], TN)).astype(jnp.bfloat16)
+        above = row_mask(level) * (base_ref[level] - dot(rows_in, fold_ref[level]))
+    out_ref[0] = above.astype(jnp.bfloat16)
 
     for phase in range(2 * (levels - 1)):
         for side, count in ((0, owners - 1), (1, owners)):
@@ -245,6 +256,12 @@
                 slot_in.at[phase, side, pl.ds(0, count)],
                 slot_send.at[phase],
             ).wait()
+
+
+def finish(in_ref, out_ref, sem):
+    copy = pltpu.make_async_copy(in_ref, out_ref, sem)
+    copy.start()
+    copy.wait()
 
 
 def shards(right_sides, inverses, couplings, widths, targets):
@@ -256,28 +273,39 @@
     lanes = rows // pieces * cols
     phases = 2 * (levels - 1)
     slot_rows = 2 * owners * SLOTS
-    hbm = pl.BlockSpec(memory_space=pl.ANY)
+    hbm = pl.BlockSpec(memory_space=pltpu.HBM)
     out = pl.pallas_call(
         functools.partial(kernel, (4, 8, 2)),
         out_shape=jax.ShapeDtypeStruct((levels, cols, width), jnp.bfloat16),
-        in_specs=[hbm, hbm, hbm, pl.BlockSpec(memory_space=pltpu.SMEM), hbm],
+        in_specs=[hbm] * 5,
         out_specs=pl.BlockSpec(memory_space=pltpu.VMEM),
         scratch_shapes=[
+            pltpu.SMEM((1, levels), jnp.int32),
             pltpu.VMEM((levels, cols, width), jnp.bfloat16),
             pltpu.VMEM((levels, width, width), jnp.bfloat16),
             pltpu.VMEM((levels - 1, rows, width), jnp.bfloat16),
             pltpu.VMEM((levels - 1, 2, owners, pieces), jnp.int32),
             pltpu.VMEM((levels - 1, slot_rows, rows), jnp.bfloat16),
             pltpu.VMEM((levels - 1, slot_rows, width), jnp.bfloat16),
+            pltpu.VMEM((levels - 1, rows, width), jnp.bfloat16),
+            pltpu.VMEM((levels - 1, cols, width), jnp.float32),
             pltpu.VMEM((phases, 2, owners, SLOTS, lanes), jnp.bfloat16),
             pltpu.VMEM((phases, 2, owners, SLOTS, lanes), jnp.bfloat16),
-            pltpu.SemaphoreType.DMA((4 * levels - 2,)),
+            pltpu.SemaphoreType.DMA((4 * levels - 1,)),
             pltpu.SemaphoreType.DMA((phases,)),
             pltpu.SemaphoreType.DMA((phases,)),
             pltpu.SemaphoreType.REGULAR,
         ],
-        compiler_params=pltpu.CompilerParams(collective_id=0, has_side_effects=True),
-    )(right, inverse, coupling, widths[0], targets)
+        compiler_params=pltpu.CompilerParams(collective_id=0, has_side_effects=True, vmem_limit_bytes=24 * 2**20),
+    )(*[pltpu.with_memory_space_constraint(v, pltpu.HBM) for v in (right, inverse, coupling)], *[pltpu.with_memory_space_constraint(v, pltpu.HBM) for v in (widths[0], targets)])
+    out = pl.pallas_call(
+        finish,
+        out_shape=jax.ShapeDtypeStruct((levels, cols, width), jnp.bfloat16),
+        in_specs=[pl.BlockSpec(memory_space=pltpu.VMEM)],
+        out_specs=pl.BlockSpec(memory_space=pltpu.HBM),
+        scratch_shapes=[pltpu.SemaphoreType.DMA],
+        compiler_params=pltpu.CompilerParams(vmem_limit_bytes=4 * 2**20),
+    )(out)
     return jnp.swapaxes(out, 1, 2)[None, None]
 
 

time: 70.8 us -> 67.5 us (0.953)
  Pallas kernels: 69.1 us -> 67.4 us
  local copies, waits for them, and re-layouts: 1.57 us -> 0 us
    pallas_call x1, Pallas kernels: 69.1 us -> 66.7 us  [shards(): pl.pallas_call(functools.partial(kernel, (4, 8, 2)), out_shape=jax.ShapeD...]
    unnamed x1 -> x0, local copies, waits for them, and re-layouts: 1.57 us -> none
where the time goes in v3:
time: 67.5 us; the launch traced here: 67.4 us
  Pallas kernels  67.4 us (100%)
    pallas_call x1, Pallas kernels, shards(): pl.pallas_call(functools.partial(kernel, (4, 8, 2)), out_shape=jax.ShapeD...  66.7 us

profile of v3, /device:TPU:1, one launch (start us, length us, event | category | flops | bytes accessed | tf_op | source)
XLA Modules:
  0.0 67.4 jit_solution(11467730744196800180)
XLA Ops:
  0.0 66.7 %shard_map.55.in_ref = bf16[4,32,512]{2,1,0:T(8,128)(2,1)S(1)} custom-call(bf16[4,32,512]{2,1,0:T(8,128)(2,1)} %bitcast.11, bf16[4,512,512]{2,1,0:T(8,128)(2,1)} %bitcast.9, bf16[3,256,512]{2,1,0:T(8,128)(2,1)} %bitcast.10, s32[1,4]{1,0:T(1,128)} %bitcast.12, s32[3,8,64,64]{3,2,1,0:T(8,128)} %tgt_hbm.1), custom_call_target="tpu_custom_call" | custom-call | tf_op jit(solution)/shard_map/pallas_call | solution.py:277
  66.7 0.7 shard_map.56

commit v4 on v3

--- a/solution.py
+++ b/solution.py
@@ -173,23 +173,33 @@
         slot_out[phase] = value.astype(jnp.bfloat16).reshape(2, owners, SLOTS, lanes)
         partner = partner_of(level)
 
-        def send(owner, last):
-            for side in (1, 0):
-                if side == 0 and last:
-                    pltpu.make_async_copy(
-                        slot_out.at[phase, 0, me], slot_in.at[phase, 0, me], slot_recv.at[phase]
-                    ).start()
-                    continue
-                pltpu.make_async_remote_copy(
-                    src_ref=slot_out.at[phase, side, owner],
-                    dst_ref=slot_in.at[phase, side, me],
-                    send_sem=slot_send.at[phase],
-                    recv_sem=slot_recv.at[phase],
-                    device_id=(partner if side else group, owner),
-                    device_id_type=MESH,
+        def send(side, owner, last):
+            if side == 0 and last:
+                pltpu.make_async_copy(
+                    slot_out.at[phase, 0, me], slot_in.at[phase, 0, me], slot_recv.at[phase]
                 ).start()
-
-        each_owner(me, sizes, send)
+                return
+            pltpu.make_async_remote_copy(
+                src_ref=slot_out.at[phase, side, owner],
+                dst_ref=slot_in.at[phase, side, me],
+                send_sem=slot_send.at[phase],
+                recv_sem=slot_recv.at[phase],
+                device_id=(partner if side else group, owner),
+                device_id_type=MESH,
+            ).start()
+
+        def send_both(owner, last):
+            send(1, owner, last)
+            send(0, owner, last)
+
+        if phase == 0:
+            pl.semaphore_wait(barrier, owners - 1 + levels - 1)
+            signal(near_sem, partner, me)
+            each_owner(me, sizes, functools.partial(send, 0))
+            pl.semaphore_wait(near_sem, 1)
+            each_owner(me, sizes, functools.partial(send, 1))
+        else:
+            each_owner(me, sizes, send_both)
 
     def slots_arrived(phase):
         pltpu.make_async_copy(slot_out.at[phase], slot_in.at[phase], slot_recv.at[phase]).wait()
@@ -214,18 +224,14 @@
     solved = forward_of(0, b_ref[0])
     cpl_loads[0].wait()
     blocks = dot(solved, cpl_ref[0], NT)
-    base_ref[0] = settled(0, solved)
     for level in range(top):
-        buffer = dot(send_mat[level], spread(blocks), NT)
-        if level == 0:
-            pl.semaphore_wait(barrier, owners - 1 + levels - 1)
-            signal(near_sem, partner_of(0), me)
-            pl.semaphore_wait(near_sem, 1)
+        buffer = jnp.transpose(dot(spread(blocks), send_mat[level], NT))
         send_slots(level, level, buffer)
         if level == 0:
             for load in loads[2:] + inv_loads[1:] + cpl_loads[1:]:
                 load.wait()
             fold(0)
+            base_ref[0] = settled(0, solved)
         else:
             base_ref[level] = settled(level, forward_of(level, residual))
         make_take(level)
@@ -243,7 +249,7 @@
         phase = top + level
         above = above.astype(jnp.bfloat16)
         out_ref[level + 1] = above
-        send_slots(phase, level, dot(take_mat[level], spread(above.astype(jnp.float32)), NT))
+        send_slots(phase, level, jnp.transpose(dot(spread(above.astype(jnp.float32)), take_mat[level], NT)))
         arrived = slots_arrived(phase)
         rows_in = collect(dot(arrived, send_mat[level], TN)).astype(jnp.bfloat16)
         above = row_mask(level) * (base_ref[level] - dot(rows_in, fold_ref[level]))

time: 67.5 us -> 66.7 us (0.988)
  Pallas kernels: 67.4 us -> 66.6 us
    pallas_call x1, Pallas kernels: 66.7 us -> 65.9 us  [shards(): pl.pallas_call(functools.partial(kernel, (4, 8, 2)), out_shape=jax.ShapeD...]
where the time goes in v4:
time: 66.7 us; the launch traced here: 66.6 us
  Pallas kernels  66.6 us (100%)
    pallas_call x1, Pallas kernels, shards(): pl.pallas_call(functools.partial(kernel, (4, 8, 2)), out_shape=jax.ShapeD...  65.9 us

profile of v4, /device:TPU:1, one launch (start us, length us, event | category | flops | bytes accessed | tf_op | source)
XLA Modules:
  0.0 66.6 jit_solution(4998205861533460490)
XLA Ops:
  0.0 65.9 %shard_map.55.in_ref = bf16[4,32,512]{2,1,0:T(8,128)(2,1)S(1)} custom-call(bf16[4,32,512]{2,1,0:T(8,128)(2,1)} %bitcast.11, bf16[4,512,512]{2,1,0:T(8,128)(2,1)} %bitcast.9, bf16[3,256,512]{2,1,0:T(8,128)(2,1)} %bitcast.10, s32[1,4]{1,0:T(1,128)} %bitcast.12, s32[3,8,64,64]{3,2,1,0:T(8,128)} %tgt_hbm.1), custom_call_target="tpu_custom_call" | custom-call | tf_op jit(solution)/shard_map/pallas_call | solution.py:283
  65.9 0.7 shard_map.56

commit v5 on v4

--- a/solution.py
+++ b/solution.py
@@ -66,6 +66,7 @@
     tbl_ref,
     send_mat,
     take_mat,
+    take_rows,
     fold_ref,
     base_ref,
     slot_out,
@@ -155,6 +156,7 @@
         spot = jnp.sum(jnp.where(count == slot_rank, spot, 0.0), axis=1, keepdims=True)
         at = (iota((1, width), 1) // piece_rows + 1).astype(jnp.float32)
         take_mat[level] = one_hot(spot == at)
+        take_rows[level] = jnp.transpose(take_mat[level])
 
     def spread(value):
         turn = iota(value.shape, 1) % piece_rows
@@ -249,7 +251,7 @@
         phase = top + level
         above = above.astype(jnp.bfloat16)
         out_ref[level + 1] = above
-        send_slots(phase, level, jnp.transpose(dot(spread(above.astype(jnp.float32)), take_mat[level], NT)))
+        send_slots(phase, level, jnp.transpose(dot(spread(above.astype(jnp.float32)), take_rows[level])))
         arrived = slots_arrived(phase)
         rows_in = collect(dot(arrived, send_mat[level], TN)).astype(jnp.bfloat16)
         above = row_mask(level) * (base_ref[level] - dot(rows_in, fold_ref[level]))
@@ -293,6 +295,7 @@
             pltpu.VMEM((levels - 1, 2, owners, pieces), jnp.int32),
             pltpu.VMEM((levels - 1, slot_rows, rows), jnp.bfloat16),
             pltpu.VMEM((levels - 1, slot_rows, width), jnp.bfloat16),
+            pltpu.VMEM((levels - 1, width, slot_rows), jnp.bfloat16),
             pltpu.VMEM((levels - 1, rows, width), jnp.bfloat16),
             pltpu.VMEM((levels - 1, cols, width), jnp.float32),
             pltpu.VMEM((phases, 2, owners, SLOTS, lanes), jnp.bfloat16),

time: 66.7 us -> 66.6 us (level)
  no operation moved by 1% of the time
where the time goes in v5:
time: 66.6 us; the launch traced here: 66.5 us
  Pallas kernels  66.5 us (100%)
    pallas_call x1, Pallas kernels, shards(): pl.pallas_call(functools.partial(kernel, (4, 8, 2)), out_shape=jax.ShapeD...  65.8 us

profile of v5, /device:TPU:1, one launch (start us, length us, event | category | flops | bytes accessed | tf_op | source)
XLA Modules:
  0.0 66.5 jit_solution(14567909694361885938)
XLA Ops:
  0.0 65.8 %shard_map.55.in_ref = bf16[4,32,512]{2,1,0:T(8,128)(2,1)S(1)} custom-call(bf16[4,32,512]{2,1,0:T(8,128)(2,1)} %bitcast.11, bf16[4,512,512]{2,1,0:T(8,128)(2,1)} %bitcast.9, bf16[3,256,512]{2,1,0:T(8,128)(2,1)} %bitcast.10, s32[1,4]{1,0:T(1,128)} %bitcast.12, s32[3,8,64,64]{3,2,1,0:T(8,128)} %tgt_hbm.1), custom_call_target="tpu_custom_call" | custom-call | tf_op jit(solution)/shard_map/pallas_call | solution.py:285
  65.8 0.7 %shard_map.56 = bf16[4,32,512]{2,1,0:T(8,128)(2,1)} custom-call(bf16[4,32,512]{2,1,0:T(8,128)(2,1)S(1)} %shard_map.55.in_ref), custom_call_target="tpu_custom_call" | custom-call | tf_op jit(solution)/shard_map/pallas_call | solution.py:310

commit v6 on v5

--- a/solution.py
+++ b/solution.py
@@ -102,14 +102,14 @@
             )
     base = 2 * levels - 1
     inv_loads = [
-        pltpu.make_async_copy(inv_hbm.at[n], inv_ref.at[n], load_sem.at[base + n])
-        for n in range(levels)
+        pltpu.make_async_copy(inv_hbm.at[part], inv_ref.at[part], load_sem.at[base + n])
+        for n, part in enumerate((pl.ds(0, 1), pl.ds(1, levels - 1)))
     ]
     cpl_loads = [
-        pltpu.make_async_copy(cpl_hbm.at[n], cpl_ref.at[n], load_sem.at[base + levels + n])
-        for n in range(levels - 1)
+        pltpu.make_async_copy(cpl_hbm.at[part], cpl_ref.at[part], load_sem.at[base + 2 + n])
+        for n, part in enumerate((pl.ds(0, 1), pl.ds(1, levels - 2)))
     ]
-    wid_load = pltpu.make_async_copy(wid_hbm, wid_ref, load_sem.at[base + 2 * levels - 1])
+    wid_load = pltpu.make_async_copy(wid_hbm, wid_ref, load_sem.at[base + 4])
     loads[1].start()
     loads[0].start()
     wid_load.start()
@@ -300,7 +300,7 @@
             pltpu.VMEM((levels - 1, cols, width), jnp.float32),
             pltpu.VMEM((phases, 2, owners, SLOTS, lanes), jnp.bfloat16),
             pltpu.VMEM((phases, 2, owners, SLOTS, lanes), jnp.bfloat16),
-            pltpu.SemaphoreType.DMA((4 * levels - 1,)),
+            pltpu.SemaphoreType.DMA((2 * levels + 4,)),
             pltpu.SemaphoreType.DMA((phases,)),
             pltpu.SemaphoreType.DMA((phases,)),
             pltpu.SemaphoreType.REGULAR,

time: 66.6 us -> 66.5 us (level)
  no operation moved by 1% of the time
where the time goes in v6:
time: 66.5 us; the launch traced here: 66.4 us
  Pallas kernels  66.4 us (100%)
    pallas_call x1, Pallas kernels, shards(): pl.pallas_call(functools.partial(kernel, (4, 8, 2)), out_shape=jax.ShapeD...  65.7 us

profile of v6, /device:TPU:1, one launch (start us, length us, event | category | flops | bytes accessed | tf_op | source)
XLA Modules:
  0.0 66.4 jit_solution(17131425689266287077)
XLA Ops:
  0.0 65.7 %shard_map.55.in_ref = bf16[4,32,512]{2,1,0:T(8,128)(2,1)S(1)} custom-call(bf16[4,32,512]{2,1,0:T(8,128)(2,1)} %bitcast.11, bf16[4,512,512]{2,1,0:T(8,128)(2,1)} %bitcast.9, bf16[3,256,512]{2,1,0:T(8,128)(2,1)} %bitcast.10, s32[1,4]{1,0:T(1,128)} %bitcast.12, s32[3,8,64,64]{3,2,1,0:T(8,128)} %tgt_hbm.1), custom_call_target="tpu_custom_call" | custom-call | tf_op jit(solution)/shard_map/pallas_call | solution.py:285
  65.7 0.7 %shard_map.56 = bf16[4,32,512]{2,1,0:T(8,128)(2,1)} custom-call(bf16[4,32,512]{2,1,0:T(8,128)(2,1)S(1)} %shard_map.55.in_ref), custom_call_target="tpu_custom_call" | custom-call | tf_op jit(solution)/shard_map/pallas_call | solution.py:310
